TPU v7x, 32 devices: a whole 2x2x4 slice. The times are simulated.
32 devices in a mesh: row: 4 (over x, core), col: 8 (over z, y).
Axes of the slice: x: 2, y: 2, z: 4, core: 2. Of those that a mesh axis runs over, the one named last changes fastest.
Arguments:
- iterate: bfloat16 [4096, 8192], P('row', 'col'), may hold values from -0.5 to 0.5, as said below
Outputs:
- update: float32 [4096, 8192], P('row', 'col')
Inputs may be any that keep to these rules, and one draw needn't show every extreme that they name: One iterate of the orthogonalization.
All inputs are finite; a program needn't handle non-finite values.
Results may differ from a plain program's by a relative error of at most 0.0041.
Values may be sent and summed in bfloat16 or wider, within the bound.
A program may use at most 64 MiB of HBM per device.

v0:
```python
import math
import jax
import jax.numpy as jnp
from jax import lax
from jax.sharding import PartitionSpec as P

COLS = 8192
coef_a = 3.4445
coef_b = -4.775
coef_c = 2.0315


def per_device(iterate):
    cols_x = lax.all_gather(iterate, "row", axis=0, tiled=True)
    mirrored = lax.psum_scatter(
        lax.dot_general(
            cols_x, iterate, (((1,), (1,)), ((), ())), preferred_element_type=jnp.float32
        ),
        "col",
        scatter_dimension=0,
        tiled=True,
    )
    gram_block = mirrored.T.astype(jnp.bfloat16)
    gram_cols = lax.all_gather(gram_block, "row", axis=0, tiled=True)
    lower = gram_cols
    square = jnp.dot(
        lax.all_gather(gram_block, "col", axis=1, tiled=True),
        lower,
        preferred_element_type=jnp.float32,
    )
    poly = (coef_b * gram_block.astype(jnp.float32) + coef_c * square).astype(jnp.bfloat16)
    lower = cols_x
    mixed = jnp.dot(
        lax.all_gather(poly, "col", axis=1, tiled=True), lower, preferred_element_type=jnp.float32
    )
    return math.sqrt(COLS) * (coef_a * iterate.astype(jnp.float32) + mixed)


def solution(mesh):
    placed = (P("row", "col"),)
    return jax.shard_map(
        per_device, mesh=mesh, in_specs=placed, out_specs=P("row", "col"), check_vma=False
    )
```

profile of v0, /device:TPU:0, one launch (start us, length us, event | category | flops | bytes accessed | tf_op | source)
XLA Modules:
  0.0 684.1 jit_solution(4347285785540661950)
XLA Ops:
  6.5 0.0 all-gather.5.cloned.1.call-start
  6.5 0.7 all-gather.5.cloned.1.call-update
  7.3 0.0 reduce-scatter.2.cloned.1.call-start
  7.3 62.6 %all-gather.5.cloned.1.call-done = bf16[4096,1024]{1,0:T(8,128)(2,1)} async-done(((bf16[1024,1024]{1,0:T(8,128)(2,1)}), bf16[4096,1024]{1,0:T(8,128)(2,1)}) %all-gather.5.cloned.1.call-update) | async-done | bytes 8388624 | tf_op jit(solution)/shard_map/all_gather | solution.py:14
  69.9 16.1 %fusion = f32[4096,1024]{1,0:T(8,128)} fusion(bf16[4096,1024]{1,0:T(8,128)(2,1)} %all-gather.5.cloned.1.call-done, bf16[1024,1024]{1,0:T(8,128)(2,1)} %param.1), kind=kOutput, calls=%fused_computation.3 | convolution fusion | flops 8589934592 | bytes 27262976 | tf_op jit(solution)/shard_map/dot_general | solution.py:16
  86.1 0.0 reduce-scatter.2.cloned.1.call-update
  86.1 0.0 all-gather.9.cloned.1.call-start
  86.1 280.3 %reduce-scatter.2.cloned.1.call-done = f32[512,1024]{1,0:T(8,128)} async-done(((f32[4096,1024]{1,0:T(8,128)}), f32[512,1024]{1,0:T(8,128)}) %reduce-scatter.2.cloned.1.call-update) | async-done | bytes 2097168 | tf_op jit(solution)/shard_map/reduce_scatter | solution.py:15
  366.5 2.7 convert_bitcast_fusion
  369.2 0.0 all-gather.9.cloned.1.call-update
  369.2 0.0 all-gather.7.cloned.1.call-start
  369.2 0.5 all-gather.7.cloned.1.call-update
  369.8 0.0 copy-start
  369.8 0.0 all-gather.11.cloned.1.call-start
  369.8 33.1 %all-gather.9.cloned.1.call-done = bf16[4096,512]{0,1:T(8,128)(2,1)} async-done(((bf16[1024,512]{0,1:T(8,128)(2,1)}), bf16[4096,512]{0,1:T(8,128)(2,1)}) %all-gather.9.cloned.1.call-update) | async-done | bytes 4194320 | tf_op jit(solution)/shard_map/all_gather | solution.py:24
  402.9 126.5 %all-gather.7.cloned.1.call-done = bf16[1024,4096]{0,1:T(8,128)(2,1)} async-done(((bf16[1024,512]{0,1:T(8,128)(2,1)}), bf16[1024,4096]{0,1:T(8,128)(2,1)}) %all-gather.7.cloned.1.call-update) | async-done | bytes 8388624 | tf_op jit(solution)/shard_map/all_gather | solution.py:27
  529.4 10.3 %add_convert_fusion = bf16[1024,512]{0,1:T(8,128)(2,1)} fusion(bf16[1024,512]{0,1:T(8,128)(2,1)} %convert_bitcast_fusion, bf16[4096,512]{0,1:T(8,128)(2,1)} %all-gather.9.cloned.1.call-done, bf16[1024,4096]{0,1:T(8,128)(2,1)} %all-gather.7.cloned.1.call-done), kind=kOutput, calls=%fused_computation.1 | convolution fusion | flops 4297588736 | bytes 14680064 | tf_op jit(solution)/shard_map/dot_general | solution.py:26
  539.7 0.0 all-gather.11.cloned.1.call-update
  539.7 122.8 %all-gather.11.cloned.1.call-done = bf16[1024,4096]{0,1:T(8,128)(2,1)} async-done(((bf16[1024,512]{0,1:T(8,128)(2,1)}), bf16[1024,4096]{0,1:T(8,128)(2,1)}) %all-gather.11.cloned.1.call-update) | async-done | bytes 8388624 | tf_op jit(solution)/shard_map/all_gather | solution.py:34
  662.5 0.0 copy-done
  662.5 15.1 %add_multiply_fusion = f32[1024,1024]{1,0:T(8,128)} fusion(bf16[1024,1024]{1,0:T(8,128)(2,1)S(1)} %copy-done, bf16[1024,4096]{0,1:T(8,128)(2,1)} %all-gather.11.cloned.1.call-done, bf16[4096,1024]{1,0:T(8,128)(2,1)} %all-gather.5.cloned.1.call-done), kind=kOutput, calls=%fused_computation | convolution fusion | flops 8594128896 | bytes 23068672 | tf_op jit(solution)/shard_map/dot_general | solution.py:33
Async XLA Ops:
  6.5 63.4 %all-gather.5.cloned.1.call-start = ((), (), s32[]{:S(2)}) async-start(), calls=%async_computation.1 | async-start | bytes 10485760 | tf_op jit(solution)/shard_map/all_gather | solution.py:14
  7.3 359.2 %reduce-scatter.2.cloned.1.call-start = ((), (), s32[]{:S(2)}) async-start(), calls=%async_computation.2 | async-start | bytes 18874368 | tf_op jit(solution)/shard_map/reduce_scatter | solution.py:15
  86.1 316.8 %all-gather.9.cloned.1.call-start = ((), (), s32[]{:S(2)}) async-start(), calls=%async_computation.4 | async-start | bytes 5242880 | tf_op jit(solution)/shard_map/all_gather | solution.py:24
  369.2 160.2 %all-gather.7.cloned.1.call-start = ((), (), s32[]{:S(2)}) async-start(), calls=%async_computation.3 | async-start | bytes 9437184 | tf_op jit(solution)/shard_map/all_gather | solution.py:27
  369.8 292.8 %copy-start = (bf16[1024,1024]{1,0:T(8,128)(2,1)S(1)}, bf16[1024,1024]{1,0:T(8,128)(2,1)}, u32[]{:S(2)}) copy-start(bf16[1024,1024]{1,0:T(8,128)(2,1)} %param.1) | copy-start | bytes 6291460
  369.8 292.7 %all-gather.11.cloned.1.call-start = ((), (), s32[]{:S(2)}) async-start(), calls=%async_computation.5 | async-start | bytes 9437184 | tf_op jit(solution)/shard_map/all_gather | solution.py:34
Sparse Core Ops, SparseCore 0:
  8.9 60.9 all-gather.4
  86.2 280.2 reduce-scatter.1
  369.3 33.5 all-gather.8
  404.9 124.4 all-gather.6
  539.8 122.6 all-gather.10
where the time goes:
time: 684 us
  waiting for transfers between devices  627 us (92%)
  matrix products  41.5 us (6%)
  between operations  13.1 us (2%)
    reduce_scatter x1, waiting for transfers between devices, per_device(): lax.psum_scatter(lax.dot_general(cols_x, iterate, (((1,), (1,)), ((), ())...  280 us
    all_gather x1, waiting for transfers between devices, per_device(): lax.all_gather(gram_block, 'col', axis=1, tiled=True)  126 us
    all_gather x1, waiting for transfers between devices, per_device(): lax.all_gather(poly, 'col', axis=1, tiled=True)  123 us
    all_gather x1, waiting for transfers between devices, per_device(): cols_x = lax.all_gather(iterate, 'row', axis=0, tiled=True)  62.6 us
    all_gather x1, waiting for transfers between devices, per_device(): gram_cols = lax.all_gather(gram_block, 'row', axis=0, tiled=True)  33.1 us
    dot_general x1, matrix products, per_device(): lax.dot_general(cols_x, iterate, (((1,), (1,)), ((), ())), preferred_elem...  16.1 us
    dot_general x1, matrix products, per_device(): jnp.dot(lax.all_gather(poly, 'col', axis=1, tiled=True), lower, preferred...  15.1 us
  transfers between devices with their start and end apart: 5, of which 5 were waited for; matrix products, arithmetic and copies ran while one was open for 0% of the time, Pallas kernels for 0%

commit v1 on v0

--- a/solution.py
+++ b/solution.py
@@ -11,7 +11,15 @@
 
 
 def per_device(iterate):
-    cols_x = lax.all_gather(iterate, "row", axis=0, tiled=True)
+    ways, here = (lax.axis_size("row"), lax.axis_index("row"))
+    grown, reach = (iterate, 1)
+    while reach < ways:
+        theirs = lax.ppermute(grown, "row", [(d, d ^ reach) for d in range(ways)])
+        mine_first = jnp.concatenate([grown, theirs], axis=0)
+        theirs_first = jnp.concatenate([theirs, grown], axis=0)
+        grown = jnp.where(here & reach == 0, mine_first, theirs_first)
+        reach = 2 * reach
+    cols_x = grown
     mirrored = lax.psum_scatter(
         lax.dot_general(
             cols_x, iterate, (((1,), (1,)), ((), ())), preferred_element_type=jnp.float32

time: 684 us -> 732 us (1.070)
  waiting for transfers between devices: 627 us -> 660 us
    ppermute x0 -> x2, waiting for transfers between devices: none -> 95.3 us  [per_device(): theirs = lax.ppermute(grown, 'row', [(d, d ^ reach) for d in range(ways)])]
    all_gather x1 -> x0, waiting for transfers between devices: 62.6 us -> none  [per_device(): cols_x = lax.all_gather(iterate, 'row', axis=0, tiled=True)]
  transfers between devices with their start and end apart: 5 -> 6, of which waited for: 5 -> 6; matrix products, arithmetic and copies ran while one was open for 0% -> 0% of each run, Pallas kernels for 0% -> 0%
where the time goes in v1:
time: 732 us
  waiting for transfers between devices  660 us (90%)
  matrix products  47.2 us (6%)
  between operations  13.1 us (2%)
  other arithmetic  8.19 us (1%)
    reduce_scatter x1, waiting for transfers between devices, per_device(): lax.psum_scatter(lax.dot_general(cols_x, iterate, (((1,), (1,)), ((), ())...  282 us
    all_gather x1, waiting for transfers between devices, per_device(): lax.all_gather(gram_block, 'col', axis=1, tiled=True)  127 us
    all_gather x1, waiting for transfers between devices, per_device(): lax.all_gather(poly, 'col', axis=1, tiled=True)  123 us
    ppermute x2, waiting for transfers between devices, per_device(): theirs = lax.ppermute(grown, 'row', [(d, d ^ reach) for d in range(ways)])  95.3 us
    all_gather x1, waiting for transfers between devices, per_device(): gram_cols = lax.all_gather(gram_block, 'row', axis=0, tiled=True)  32.8 us
    dot_general x1, matrix products, per_device(): lax.dot_general(cols_x, iterate, (((1,), (1,)), ((), ())), preferred_elem...  20.5 us
    dot_general x1, matrix products, per_device(): jnp.dot(lax.all_gather(poly, 'col', axis=1, tiled=True), lower, preferred...  16.4 us
  transfers between devices with their start and end apart: 6, of which 6 were waited for; matrix products, arithmetic and copies ran while one was open for 0% of the time, Pallas kernels for 0%

profile of v1, /device:TPU:0, one launch (start us, length us, event | category | flops | bytes accessed | tf_op | source)
XLA Modules:
  0.0 732.2 jit_solution(7588960164413900109)
XLA Ops:
  6.5 0.0 reduce-scatter.2.cloned.1.call-start
  6.5 0.5 collective-permute-start
  7.0 0.0 copy-start
  7.0 4.1 collective-permute-done
  11.2 5.5 maximum_select_fusion.1
  16.6 2.8 collective-permute-start.1
  19.5 91.2 %collective-permute-done.1 = bf16[2048,1024]{1,0:T(8,128)(2,1)} collective-permute-done((bf16[2048,1024]{1,0:T(8,128)(2,1)}, bf16[2048,1024]{1,0:T(8,128)(2,1)}, u32[]{:S(2)}, u32[]{:S(2)}) %collective-permute-start.1) | collective-permute-done | bytes 4194336 | tf_op jit(solution)/shard_map/ppermute | solution.py:17
  110.7 0.0 copy-done
  110.7 20.5 %fusion = f32[4096,1024]{1,0:T(8,128)} fusion(bf16[1024,1024]{1,0:T(8,128)(2,1)S(1)} %copy-done, bf16[2048,1024]{1,0:T(8,128)(2,1)} %collective-permute-done.1, bf16[2048,1024]{1,0:T(8,128)(2,1)} %maximum_select_fusion.1, pred[]{:T(512)S(6)} %eq.6), kind=kOutput, calls=%fused_computation.4 | convolution fusion | flops 8627683328 | bytes 27262976 | tf_op jit(solution)/shard_map/dot_general | solution.py:24
  131.2 0.0 reduce-scatter.2.cloned.1.call-update
  131.2 0.0 all-gather.6.cloned.1.call-start
  131.3 281.8 %reduce-scatter.2.cloned.1.call-done = f32[512,1024]{1,0:T(8,128)} async-done(((f32[4096,1024]{1,0:T(8,128)}), f32[512,1024]{1,0:T(8,128)}) %reduce-scatter.2.cloned.1.call-update) | async-done | bytes 2097168 | tf_op jit(solution)/shard_map/reduce_scatter | solution.py:23
  413.0 2.7 convert_bitcast_fusion
  415.8 0.0 all-gather.6.cloned.1.call-update
  415.8 0.0 all-gather.4.cloned.1.call-start
  415.8 0.7 all-gather.4.cloned.1.call-update
  416.5 0.2 all-gather.8.cloned.1.call-start
  416.7 32.8 %all-gather.6.cloned.1.call-done = bf16[4096,512]{0,1:T(8,128)(2,1)} async-done(((bf16[1024,512]{0,1:T(8,128)(2,1)}), bf16[4096,512]{0,1:T(8,128)(2,1)}) %all-gather.6.cloned.1.call-update) | async-done | bytes 4194320 | tf_op jit(solution)/shard_map/all_gather | solution.py:32
  449.5 126.6 %all-gather.4.cloned.1.call-done = bf16[1024,4096]{0,1:T(8,128)(2,1)} async-done(((bf16[1024,512]{0,1:T(8,128)(2,1)}), bf16[1024,4096]{0,1:T(8,128)(2,1)}) %all-gather.4.cloned.1.call-update) | async-done | bytes 8388624 | tf_op jit(solution)/shard_map/all_gather | solution.py:35
  576.1 10.3 %add_convert_fusion = bf16[1024,512]{0,1:T(8,128)(2,1)} fusion(bf16[1024,512]{0,1:T(8,128)(2,1)} %convert_bitcast_fusion, bf16[4096,512]{0,1:T(8,128)(2,1)} %all-gather.6.cloned.1.call-done, bf16[1024,4096]{0,1:T(8,128)(2,1)} %all-gather.4.cloned.1.call-done), kind=kOutput, calls=%fused_computation.3 | convolution fusion | flops 4297588736 | bytes 14680064 | tf_op jit(solution)/shard_map/dot_general | solution.py:34
  586.4 0.0 all-gather.8.cloned.1.call-update
  586.5 122.8 %all-gather.8.cloned.1.call-done = bf16[1024,4096]{0,1:T(8,128)(2,1)} async-done(((bf16[1024,512]{0,1:T(8,128)(2,1)}), bf16[1024,4096]{0,1:T(8,128)(2,1)}) %all-gather.8.cloned.1.call-update) | async-done | bytes 8388624 | tf_op jit(solution)/shard_map/all_gather | solution.py:42
  709.3 16.4 %add_multiply_fusion = f32[1024,1024]{1,0:T(8,128)} fusion(bf16[1024,1024]{1,0:T(8,128)(2,1)S(1)} %copy-done, bf16[1024,4096]{0,1:T(8,128)(2,1)} %all-gather.8.cloned.1.call-done, bf16[2048,1024]{1,0:T(8,128)(2,1)} %collective-permute-done.1, bf16[2048,1024]{1,0:T(8,128)(2,1)} %maximum_select_fusion.1, pred[]{:T(512)S(6)} %eq.6), kind=kOutput, calls=%fused_computation.2 | convolution fusion | flops 8631877632 | bytes 23068672 | tf_op jit(solution)/shard_map/dot_general | solution.py:41
Async XLA Ops:
  6.5 406.5 %reduce-scatter.2.cloned.1.call-start = ((), (), s32[]{:S(2)}) async-start(), calls=%async_computation.1 | async-start | bytes 18874368 | tf_op jit(solution)/shard_map/reduce_scatter | solution.py:23
  6.5 4.6 collective-permute-start
  7.0 103.6 %copy-start = (bf16[1024,1024]{1,0:T(8,128)(2,1)S(1)}, bf16[1024,1024]{1,0:T(8,128)(2,1)}, u32[]{:S(2)}) copy-start(bf16[1024,1024]{1,0:T(8,128)(2,1)} %param.1) | copy-start | bytes 6291460
  16.6 94.0 %collective-permute-start.1 = (bf16[2048,1024]{1,0:T(8,128)(2,1)}, bf16[2048,1024]{1,0:T(8,128)(2,1)}, u32[]{:S(2)}, u32[]{:S(2)}) collective-permute-start(bf16[2048,1024]{1,0:T(8,128)(2,1)} %maximum_select_fusion.1), channel_id=1, source_target_pairs={{0,16},{8,24},{16,0},{24,8},{1,17},{9,25},{17,1},{25,9},{2,18},{10... | collective-permute-start | bytes 12582920 | tf_op jit(solution)/shard_map/ppermute | solution.py:17
  131.2 318.3 %all-gather.6.cloned.1.call-start = ((), (), s32[]{:S(2)}) async-start(), calls=%async_computation.3 | async-start | bytes 5242880 | tf_op jit(solution)/shard_map/all_gather | solution.py:32
  415.8 160.4 %all-gather.4.cloned.1.call-start = ((), (), s32[]{:S(2)}) async-start(), calls=%async_computation.2 | async-start | bytes 9437184 | tf_op jit(solution)/shard_map/all_gather | solution.py:35
  416.5 292.8 %all-gather.8.cloned.1.call-start = ((), (), s32[]{:S(2)}) async-start(), calls=%async_computation.4 | async-start | bytes 9437184 | tf_op jit(solution)/shard_map/all_gather | solution.py:42
Sparse Core Ops, SparseCore 0:
  131.3 281.6 reduce-scatter.1
  415.9 33.5 all-gather.5
  451.6 124.4 all-gather.3
  586.6 122.6 all-gather.7
